TPU v7x, 32 devices: a whole 2x2x4 slice. The times are simulated.
32 devices in a mesh: train: 16 (over z, y, core), cand: 2 (over x).
Axes of the slice: x: 2, y: 2, z: 4, core: 2. Of those that a mesh axis runs over, the one named last changes fastest.
Arguments:
- x_train: float32 [8, 2048], P(None, 'train'), may hold values from -4 to 4
- x_cand: float32 [8, 1024], P(None, 'cand'), may hold values from -4 to 4
- targets: float32 [2048], P(('train', 'cand')), may hold values from -6 to 6
- noise: float32 [2048, 64], P(('train', 'cand')), may hold values from -5 to 5
- omega: float32 [8, 4096], replicated, may hold values from -6 to 6
- phase: float32 [4096], replicated, may hold values from -3.140625 to 3.140625
- prior_weights: bfloat16 [4096, 64], P('cand'), may hold values from -6 to 6
Outputs:
- samples: float32 [1024, 64], P(('cand', 'train'))
- solution: float32 [2048, 64], P(('train', 'cand'))
All inputs are finite; a program needn't handle non-finite values.
Results may differ from a plain program's by a relative error of at most 0.0019.
The roundings to bfloat16 on the way count: a program that leaves them out, or rounds other values in their place, can miss the bound.
Values may be sent and summed in bfloat16 or wider, within the bound.
No kernel may reach another device: no remote copies, remote signals or barrier semaphores. Data moves between devices by JAX's collectives and lax.ppermute only.
A program may use at most 64 MiB of HBM per device.

v0:
```python
import math
import jax
import jax.numpy as jnp
from jax import lax
from jax.sharding import PartitionSpec as P

ITERS = 2
noise_level = 0.5


def squares_of(points):
    return jnp.sum(points * points, axis=0)


def kernel_tile(row_points, row_norms, column_points, column_norms):
    inner = jnp.dot(row_points.T, column_points, precision=lax.Precision.HIGHEST)
    return jnp.exp(-0.5 * (row_norms[:, None] + column_norms[None, :] - 2.0 * inner)).astype(
        jnp.bfloat16
    )


def features(points, omega, phase):
    angles = jnp.dot(points.T, omega, precision=lax.Precision.HIGHEST) + phase[None, :]
    return (math.sqrt(2.0 / omega.shape[1]) * jnp.cos(angles)).astype(jnp.bfloat16)


def kernel_rows(points, every_point, every_norm, weights):
    count = points.shape[1]
    size = math.gcd(count, 1024)
    stacked = points.reshape(points.shape[0], count // size, size).transpose(1, 0, 2)

    def one_block(block_points):
        tile = kernel_tile(block_points, squares_of(block_points), every_point, every_norm)
        return jnp.dot(tile, weights, preferred_element_type=jnp.float32)

    return lax.map(one_block, stacked).reshape(count, weights.shape[1])


def body(x_train, x_cand, targets, noise, omega, phase, prior_weights):
    own_rows = noise.shape[0]
    cand_index = lax.axis_index("cand")
    train_index = lax.axis_index("train")
    own_points = lax.dynamic_slice_in_dim(x_train, cand_index * own_rows, own_rows, 1)
    full_weights = lax.all_gather(prior_weights, "cand", axis=0, tiled=True)
    prior_train = jnp.dot(
        features(own_points, omega, phase), full_weights, preferred_element_type=jnp.float32
    )
    rhs = targets[:, None] - prior_train - noise
    column_points = lax.all_gather(own_points, "train", axis=1, tiled=True)
    row_norms = squares_of(x_train)
    column_norms = squares_of(column_points)
    width = max(128, 262144 // x_train.shape[1])

    def squares(values):
        return lax.psum(jnp.sum(values * values, axis=0), ("train", "cand"))

    solution = jnp.zeros(rhs.shape, jnp.float32)
    residual = rhs
    direction = rhs
    norm_now = squares(residual)
    for step in range(ITERS):
        packed = direction.astype(jnp.bfloat16)
        empty = jnp.zeros((x_train.shape[1], packed.shape[1]), jnp.float32)
        total = empty
        piece = lax.all_gather(packed, "train", axis=0, tiled=True)
        for offset in range(0, piece.shape[0], width):
            count = min(width, piece.shape[0] - offset)
            accumulate_points = lax.dynamic_slice_in_dim(column_points, offset, count, 1)
            norms = lax.dynamic_slice_in_dim(column_norms, offset, count, 0)
            tile = kernel_tile(x_train, row_norms, accumulate_points, norms)
            total = total + jnp.dot(
                tile, piece[offset : offset + count], preferred_element_type=jnp.float32
            )
        apply_total = total
        apply_total = lax.psum_scatter(apply_total, "cand", scatter_dimension=0, tiled=True)
        image = apply_total + noise_level * direction
        curve = lax.psum(jnp.sum(direction * image, axis=0), ("train", "cand"))
        alpha = norm_now / curve
        solution = solution + alpha * direction
        residual = residual - alpha * image
        norm_next = squares(residual)
        direction = residual + norm_next / norm_now * direction
        norm_now = norm_next
    per_device = x_cand.shape[1] // lax.axis_size("train")
    mine = lax.dynamic_slice_in_dim(x_cand, train_index * per_device, per_device, 1)
    packed_solution = solution.astype(jnp.bfloat16)
    block_weights = lax.all_gather(packed_solution, "cand", axis=0, tiled=True)
    train_norms = squares_of(x_train)
    kernel_part = lax.psum_scatter(
        kernel_rows(x_cand, x_train, train_norms, block_weights),
        "train",
        scatter_dimension=0,
        tiled=True,
    )
    prior_cand = jnp.dot(
        features(mine, omega, phase), full_weights, preferred_element_type=jnp.float32
    )
    return (prior_cand + kernel_part, solution)


def solution(mesh):
    placed = (
        P(None, "train"),
        P(None, "cand"),
        P(("train", "cand")),
        P(("train", "cand"), None),
        P(),
        P(),
        P("cand", None),
    )
    return jax.shard_map(
        body,
        mesh=mesh,
        in_specs=placed,
        out_specs=(P(("cand", "train"), None), P(("train", "cand"), None)),
        check_vma=False,
    )
```

profile of v0, /device:TPU:0, one launch (start us, length us, event | category | flops | bytes accessed | tf_op | source)
XLA Modules:
  0.0 296.1 jit_solution(272035158380049314)
XLA Ops:
  7.2 0.7 multiply_reduce_fusion.6
  8.0 10.3 %all_gather.15 = bf16[4096,64]{0,1:T(8,128)(2,1)S(1)} all-gather(bf16[2048,64]{0,1:T(8,128)(2,1)} %param.13), channel_id=1, replica_groups=mesh['train'=16,'cand'=2] {'cand'}, dimensions={0}, use_global_device_ids=true | all-gather | bytes 786432 | tf_op jit(solution)/shard_map/all_gather | solution.py:44
  18.4 22.0 %all-gather = f32[16,64,8]{1,2,0:T(8,128)S(1)} all-gather(f32[1,64,8]{1,2,0:T(8,128)S(1)} %dynamic-slice_bitcast_fusion), channel_id=1, replica_groups=mesh['train'=16,'cand'=2] {'train'}, dimensions={0}, use_global_device_ids=true | all-gather | bytes 34816 | tf_op jit(solution)/shard_map/all_gather | solution.py:49
  40.5 0.7 copy-done.2
  41.2 4.7 %fusion.2 = bf16[64,4096]{1,0:T(8,128)(2,1)S(1)} fusion(f32[8,4096]{1,0:T(8,128)S(1)} %copy-done, f32[4096]{0:T(1024)S(1)} %copy-done.2, f32[8,128]{1,0:T(8,128)S(1)} %copy-done.3, s32[]{:T(128)S(6)} %select_n.7), kind=kOutput, calls=%fused_computation.3 | convolution fusion | flops 25952256 | bytes 675844 | tf_op jit(solution)/shard_map/dot_general | solution.py:23
  46.3 18.1 %all_gather.17 = bf16[1024,64]{1,0:T(8,128)(2,1)S(1)} all-gather(bf16[64,64]{1,0:T(8,128)(2,1)S(1)} %get-tuple-element.26), channel_id=1, replica_groups=mesh['train'=16,'cand'=2] {'train'}, dimensions={0}, use_global_device_ids=true | all-gather | bytes 139264 | tf_op jit(solution)/shard_map/all_gather | solution.py:65
  64.4 1.0 fusion.10
  65.5 0.9 fusion.23
  66.5 0.6 copy-done.5
  67.1 7.8 %reduce-scatter.4.cloned.1.call-done = f32[64,64]{1,0:T(8,128)} async-done(((f32[128,64]{1,0:T(8,128)}), f32[64,64]{1,0:T(8,128)}) %reduce-scatter.4.cloned.1.call-update) | async-done | bytes 16400 | tf_op jit(solution)/shard_map/reduce_scatter | solution.py:75
  74.9 0.9 multiply_reduce_fusion.3
  75.8 39.3 %all-reduce = (f32[64]{0:T(128)S(1)}, f32[64]{0:T(128)S(1)}) all-reduce(f32[64]{0:T(128)S(1)} %get-tuple-element.15, f32[64]{0:T(128)S(1)} %get-tuple-element.14), channel_id=1, replica_groups=mesh['train'=16,'cand'=2] {'train','cand'}, use_global_device_ids=true, to_apply=%region_3.0 | all-reduce | flops 128 | bytes 1024 | tf_op jit(solution)/shard_map/psum | solution.py:55
  115.2 41.0 %psum.30 = f32[64]{0:T(128)S(1)} all-reduce(f32[64]{0:T(128)S(1)} %multiply_reduce_fusion.2), channel_id=1, replica_groups=mesh['train'=16,'cand'=2] {'train','cand'}, use_global_device_ids=true, to_apply=%region_9.0 | all-reduce | flops 64 | bytes 512 | tf_op jit(solution)/shard_map/psum | solution.py:55
  156.2 21.8 %all_gather.18 = bf16[1024,64]{1,0:T(8,128)(2,1)S(1)} all-gather(bf16[64,64]{1,0:T(8,128)(2,1)S(1)} %fusion.20), channel_id=1, replica_groups=mesh['train'=16,'cand'=2] {'train'}, dimensions={0}, use_global_device_ids=true | all-gather | bytes 139264 | tf_op jit(solution)/shard_map/all_gather | solution.py:65
  178.0 0.9 fusion.24
  179.6 5.8 %reduce-scatter.6.cloned.1.call-done = f32[64,64]{1,0:T(8,128)} async-done(((f32[128,64]{1,0:T(8,128)}), f32[64,64]{1,0:T(8,128)}) %reduce-scatter.6.cloned.1.call-update) | async-done | bytes 16400 | tf_op jit(solution)/shard_map/reduce_scatter | solution.py:75
  185.4 0.8 multiply_reduce_fusion.1
  186.1 39.3 %psum.31 = f32[64]{0:T(128)S(1)} all-reduce(f32[64]{0:T(128)S(1)} %multiply_reduce_fusion.1), channel_id=1, replica_groups=mesh['train'=16,'cand'=2] {'train','cand'}, use_global_device_ids=true, to_apply=%region_12.0 | all-reduce | flops 64 | bytes 512 | tf_op jit(solution)/shard_map/psum | solution.py:77
  225.5 0.6 fusion.21
  226.1 4.6 %all_gather.19 = bf16[128,64]{1,0:T(8,128)(2,1)S(1)} all-gather(bf16[64,64]{1,0:T(8,128)(2,1)S(1)} %get-tuple-element.24), channel_id=1, replica_groups=mesh['train'=16,'cand'=2] {'cand'}, dimensions={0}, use_global_device_ids=true | all-gather | bytes 24576 | tf_op jit(solution)/shard_map/all_gather | solution.py:87
  230.7 0.9 fusion.25
  231.6 2.7 fusion.5
  234.3 53.7 %reduce-scatter.8.cloned.1.call-done = f32[32,64]{1,0:T(8,128)} async-done(((f32[512,64]{1,0:T(8,128)}), f32[32,64]{1,0:T(8,128)}) %reduce-scatter.8.cloned.1.call-update) | async-done | bytes 8208 | tf_op jit(solution)/shard_map/reduce_scatter | solution.py:89
  288.0 1.6 convolution_add_fusion.2
  (30 shorter events, 1.4 us)
Async XLA Ops:
  7.2 33.3 %copy-start = (f32[8,4096]{1,0:T(8,128)S(1)}, f32[8,4096]{1,0:T(8,128)}, u32[]{:S(2)}) copy-start(f32[8,4096]{1,0:T(8,128)} %param.11) | copy-start | bytes 393220
  7.2 67.8 %reduce-scatter.4.cloned.1.call-start = ((), (), s32[]{:S(2)}) async-start(), calls=%async_computation.3 | async-start | bytes 98304 | tf_op jit(solution)/shard_map/reduce_scatter | solution.py:75
  8.0 10.3 %copy-start.3 = (f32[8,128]{1,0:T(8,128)S(1)}, f32[8,128]{1,0:T(8,128)}, u32[]{:S(2)}) copy-start(f32[8,128]{1,0:T(8,128)} %param.7) | copy-start | bytes 12292
  40.5 0.7 copy-start.2
  41.2 4.8 %copy-start.4 = (f32[64,64]{1,0:T(8,128)S(1)}, f32[64,64]{1,0:T(8,128)}, u32[]{:S(2)}) copy-start(f32[64,64]{1,0:T(8,128)} %param.10) | copy-start | bytes 49156
  41.2 4.8 %copy-start.6 = (f32[64]{0:T(128)S(1)}, f32[64]{0:T(128)}, u32[]{:S(2)}) copy-start(f32[64]{0:T(128)} %param.9) | copy-start | bytes 772
  66.4 0.7 copy-start.5
  66.4 119.0 %reduce-scatter.6.cloned.1.call-start = ((), (), s32[]{:S(2)}) async-start(), calls=%async_computation.4 | async-start | bytes 98304 | tf_op jit(solution)/shard_map/reduce_scatter | solution.py:75
  74.9 40.2 %copy-start.1 = (f32[64,64]{1,0:T(8,128)S(1)}, f32[64,64]{1,0:T(8,128)}, u32[]{:S(2)}) copy-start(f32[64,64]{1,0:T(8,128)} %reduce-scatter.4.cloned.1.call-done) | copy-start | bytes 49156
  178.9 109.1 %reduce-scatter.8.cloned.1.call-start = ((), (), s32[]{:S(2)}) async-start(), calls=%async_computation.5 | async-start | bytes 278528 | tf_op jit(solution)/shard_map/reduce_scatter | solution.py:89
Sparse Core Ops, SparseCore 0:
  66.5 8.3 reduce-scatter.3
  179.0 6.2 reduce-scatter.5
  231.8 56.2 reduce-scatter.7
where the time goes:
time: 297 us; the launch traced here: 296 us
  blocking collectives  197 us (66%)
  waiting for transfers between devices  67.3 us (23%)
  between operations  13.9 us (5%)
  matrix products  13.6 us (5%)
  other arithmetic  3.1 us (1%)
    psum x2, blocking collectives, squares(): return lax.psum(jnp.sum(values * values, axis=0), ('train', 'cand'))  80.3 us
    reduce_scatter x1, waiting for transfers between devices, body(): lax.psum_scatter(kernel_rows(x_cand, x_train, train_norms, block_weights)...  53.7 us
    all_gather x2, blocking collectives, body(): piece = lax.all_gather(packed, 'train', axis=0, tiled=True)  40 us
    psum x1, blocking collectives, body(): curve = lax.psum(jnp.sum(direction * image, axis=0), ('train', 'cand'))  39.3 us
    all_gather x1, blocking collectives, body(): column_points = lax.all_gather(own_points, 'train', axis=1, tiled=True)  22 us
    reduce_scatter x2, waiting for transfers between devices, body(): lax.psum_scatter(apply_total, 'cand', scatter_dimension=0, tiled=True)  13.6 us
    all_gather x1, blocking collectives, body(): full_weights = lax.all_gather(prior_weights, 'cand', axis=0, tiled=True)  10.3 us
    dot_general x2, matrix products, features(): jnp.dot(points.T, omega, precision=lax.Precision.HIGHEST) + phase[None, :]  7.44 us
  transfers between devices with their start and end apart: 3, of which 3 were waited for; matrix products, arithmetic and copies ran while one was open for 1% of the time, Pallas kernels for 0%

commit v1 on v0

--- a/solution.py
+++ b/solution.py
@@ -6,6 +6,19 @@
 
 ITERS = 2
 noise_level = 0.5
+
+
+def gather_around(shard, axis, dim):
+    ways = lax.axis_size(axis)
+    up = [(d, (d + 1) % ways) for d in range(ways)]
+    down = [(d, (d - 1) % ways) for d in range(ways)]
+    earlier, later = ([shard], [shard])
+    for _ in range(ways // 2):
+        earlier.append(lax.ppermute(earlier[-1], axis, up))
+    for _ in range((ways - 1) // 2):
+        later.append(lax.ppermute(later[-1], axis, down))
+    line = jnp.concatenate([*earlier[::-1], *later[1:]], axis=dim)
+    return jnp.roll(line, (lax.axis_index(axis) - ways // 2) * shard.shape[dim], axis=dim)
 
 
 def squares_of(points):
@@ -46,7 +59,7 @@
         features(own_points, omega, phase), full_weights, preferred_element_type=jnp.float32
     )
     rhs = targets[:, None] - prior_train - noise
-    column_points = lax.all_gather(own_points, "train", axis=1, tiled=True)
+    column_points = gather_around(own_points, "train", 1)
     row_norms = squares_of(x_train)
     column_norms = squares_of(column_points)
     width = max(128, 262144 // x_train.shape[1])

time: 297 us -> 309 us (1.040)
  starting transfers between devices: 0.12 us -> 31.2 us
  blocking collectives: 197 us -> 172 us
  waiting for transfers between devices: 67.3 us -> 73.3 us
    ppermute x0 -> x15, starting transfers between devices: none -> 31.1 us  [the longest x7 30.5 us: gather_around(): later.append(lax.ppermute(later[-1], axis, down))]
    all_gather x1 -> x0, blocking collectives: 22 us -> none  [body(): column_points = lax.all_gather(own_points, 'train', axis=1, tiled=True)]
    ppermute x0 -> x15, waiting for transfers between devices: none -> 6.22 us  [the longest x8 3.86 us: gather_around(): earlier.append(lax.ppermute(earlier[-1], axis, up))]
    all_gather x1, blocking collectives: 10.3 us -> 7.04 us  [body(): full_weights = lax.all_gather(prior_weights, 'cand', axis=0, tiled=True)]
  transfers between devices with their start and end apart: 3 -> 18, of which waited for: 3 -> 8; matrix products, arithmetic and copies ran while one was open for 1% -> 3% of each run, Pallas kernels for 0% -> 0%
where the time goes in v1:
time: 309 us; the launch traced here: 308 us
  blocking collectives  172 us (56%)
  waiting for transfers between devices  73.3 us (24%)
  starting transfers between devices  31.2 us (10%)
  between operations  13.9 us (4%)
  matrix products  13.6 us (4%)
    psum x2, blocking collectives, squares(): return lax.psum(jnp.sum(values * values, axis=0), ('train', 'cand'))  80.3 us
    reduce_scatter x1, waiting for transfers between devices, body(): lax.psum_scatter(kernel_rows(x_cand, x_train, train_norms, block_weights)...  53.7 us
    all_gather x2, blocking collectives, body(): piece = lax.all_gather(packed, 'train', axis=0, tiled=True)  40.6 us
    psum x1, blocking collectives, body(): curve = lax.psum(jnp.sum(direction * image, axis=0), ('train', 'cand'))  39.3 us
    ppermute x7, starting transfers between devices, gather_around(): later.append(lax.ppermute(later[-1], axis, down))  30.5 us
    reduce_scatter x2, waiting for transfers between devices, body(): lax.psum_scatter(apply_total, 'cand', scatter_dimension=0, tiled=True)  13.3 us
    dot_general x2, matrix products, features(): jnp.dot(points.T, omega, precision=lax.Precision.HIGHEST) + phase[None, :]  7.32 us
    all_gather x1, blocking collectives, body(): full_weights = lax.all_gather(prior_weights, 'cand', axis=0, tiled=True)  7.04 us
  transfers between devices with their start and end apart: 18, of which 8 were waited for; matrix products, arithmetic and copies ran while one was open for 3% of the time, Pallas kernels for 0%

profile of v1, /device:TPU:0, one launch (start us, length us, event | category | flops | bytes accessed | tf_op | source)
XLA Modules:
  0.0 307.9 jit_solution(14169376286104838684)
XLA Ops:
  8.5 5.0 %collective-permute-start.8 = (f32[8,64]{1,0:T(8,128)S(1)}, f32[8,64]{1,0:T(8,128)S(1)}, u32[]{:S(2)}, u32[]{:S(2)}) collective-permute-start(f32[8,64]{1,0:T(8,128)S(1)} %constant_dynamic-slice_fusion), channel_id=1, source_target_pairs={{0,30},{2,0},{4,2},{6,4},{8,6},{10,8},{12,10},{14,12},{16,14},{18,... | collective-permute-start | bytes 6152 | tf_op jit(solution)/shard_map/ppermute | solution.py:19
  13.5 1.3 collective-permute-done
  14.8 4.4 %collective-permute-start.9 = (f32[8,64]{1,0:T(8,128)S(1)}, f32[8,64]{1,0:T(8,128)S(1)}, u32[]{:S(2)}, u32[]{:S(2)}) collective-permute-start(f32[8,64]{1,0:T(8,128)S(1)} %collective-permute-done.8), channel_id=1, source_target_pairs={{0,30},{2,0},{4,2},{6,4},{8,6},{10,8},{12,10},{14,12},{16,14},{18,... | collective-permute-start | bytes 6152 | tf_op jit(solution)/shard_map/ppermute | solution.py:19
  19.2 1.3 collective-permute-done.1
  20.5 4.4 %collective-permute-start.10 = (f32[8,64]{1,0:T(8,128)S(1)}, f32[8,64]{1,0:T(8,128)S(1)}, u32[]{:S(2)}, u32[]{:S(2)}) collective-permute-start(f32[8,64]{1,0:T(8,128)S(1)} %collective-permute-done.9), channel_id=1, source_target_pairs={{0,30},{2,0},{4,2},{6,4},{8,6},{10,8},{12,10},{14,12},{16,14},{18,... | collective-permute-start | bytes 6152 | tf_op jit(solution)/shard_map/ppermute | solution.py:19
  24.9 1.3 collective-permute-done.2
  26.2 4.6 %fusion.2 = bf16[64,4096]{1,0:T(8,128)(2,1)S(1)} fusion(f32[8,64]{1,0:T(8,128)S(1)} %constant_dynamic-slice_fusion, f32[8,4096]{1,0:T(8,128)S(1)} %copy-done, f32[4096]{0:T(1024)S(1)} %copy-done.3), kind=kOutput, calls=%fused_computation.3 | convolution fusion | flops 25952256 | bytes 673792 | tf_op jit(solution)/shard_map/dot_general | solution.py:36
  30.9 4.5 %collective-permute-start.11 = (f32[8,64]{1,0:T(8,128)S(1)}, f32[8,64]{1,0:T(8,128)S(1)}, u32[]{:S(2)}, u32[]{:S(2)}) collective-permute-start(f32[8,64]{1,0:T(8,128)S(1)} %collective-permute-done.10), channel_id=1, source_target_pairs={{0,30},{2,0},{4,2},{6,4},{8,6},{10,8},{12,10},{14,12},{16,14},{18,... | collective-permute-start | bytes 6152 | tf_op jit(solution)/shard_map/ppermute | solution.py:19
  35.4 7.0 %all_gather.12 = bf16[4096,64]{0,1:T(8,128)(2,1)S(1)} all-gather(bf16[2048,64]{0,1:T(8,128)(2,1)S(1)} %copy-done.2), channel_id=1, replica_groups=mesh['train'=16,'cand'=2] {'cand'}, dimensions={0}, use_global_device_ids=true | all-gather | bytes 786432 | tf_op jit(solution)/shard_map/all_gather | solution.py:57
  42.4 3.5 %collective-permute-start.12 = (f32[8,64]{1,0:T(8,128)S(1)}, f32[8,64]{1,0:T(8,128)S(1)}, u32[]{:S(2)}, u32[]{:S(2)}) collective-permute-start(f32[8,64]{1,0:T(8,128)S(1)} %collective-permute-done.11), channel_id=1, source_target_pairs={{0,30},{2,0},{4,2},{6,4},{8,6},{10,8},{12,10},{14,12},{16,14},{18,... | collective-permute-start | bytes 6152 | tf_op jit(solution)/shard_map/ppermute | solution.py:19
  47.2 4.4 %collective-permute-start.13 = (f32[8,64]{1,0:T(8,128)S(1)}, f32[8,64]{1,0:T(8,128)S(1)}, u32[]{:S(2)}, u32[]{:S(2)}) collective-permute-start(f32[8,64]{1,0:T(8,128)S(1)} %collective-permute-done.12), channel_id=1, source_target_pairs={{0,30},{2,0},{4,2},{6,4},{8,6},{10,8},{12,10},{14,12},{16,14},{18,... | collective-permute-start | bytes 6152 | tf_op jit(solution)/shard_map/ppermute | solution.py:19
  51.7 1.3 collective-permute-done.13
  53.0 4.4 %collective-permute-start.14 = (f32[8,64]{1,0:T(8,128)S(1)}, f32[8,64]{1,0:T(8,128)S(1)}, u32[]{:S(2)}, u32[]{:S(2)}) collective-permute-start(f32[8,64]{1,0:T(8,128)S(1)} %collective-permute-done.13), channel_id=1, source_target_pairs={{0,30},{2,0},{4,2},{6,4},{8,6},{10,8},{12,10},{14,12},{16,14},{18,... | collective-permute-start | bytes 6152 | tf_op jit(solution)/shard_map/ppermute | solution.py:19
  57.4 18.8 %all_gather.13 = bf16[1024,64]{1,0:T(8,128)(2,1)S(1)} all-gather(bf16[64,64]{1,0:T(8,128)(2,1)S(1)} %get-tuple-element.26), channel_id=1, replica_groups=mesh['train'=16,'cand'=2] {'train'}, dimensions={0}, use_global_device_ids=true | all-gather | bytes 139264 | tf_op jit(solution)/shard_map/all_gather | solution.py:78
  79.1 7.5 %reduce-scatter.4.cloned.1.call-done = f32[64,64]{1,0:T(8,128)} async-done(((f32[128,64]{1,0:T(8,128)}), f32[64,64]{1,0:T(8,128)}) %reduce-scatter.4.cloned.1.call-update) | async-done | bytes 16400 | tf_op jit(solution)/shard_map/reduce_scatter | solution.py:88
  87.5 39.3 %all-reduce = (f32[64]{0:T(128)S(1)}, f32[64]{0:T(128)S(1)}) all-reduce(f32[64]{0:T(128)S(1)} %get-tuple-element.15, f32[64]{0:T(128)S(1)} %get-tuple-element.14), channel_id=1, replica_groups=mesh['train'=16,'cand'=2] {'train','cand'}, use_global_device_ids=true, to_apply=%region_3.4 | all-reduce | flops 128 | bytes 1024 | tf_op jit(solution)/shard_map/psum | solution.py:68
  126.9 41.0 %psum.30 = f32[64]{0:T(128)S(1)} all-reduce(f32[64]{0:T(128)S(1)} %multiply_reduce_fusion.1), channel_id=1, replica_groups=mesh['train'=16,'cand'=2] {'train','cand'}, use_global_device_ids=true, to_apply=%region_9.10 | all-reduce | flops 64 | bytes 512 | tf_op jit(solution)/shard_map/psum | solution.py:68
  167.9 21.8 %all_gather.14 = bf16[1024,64]{1,0:T(8,128)(2,1)S(1)} all-gather(bf16[64,64]{1,0:T(8,128)(2,1)S(1)} %fusion.20), channel_id=1, replica_groups=mesh['train'=16,'cand'=2] {'train'}, dimensions={0}, use_global_device_ids=true | all-gather | bytes 139264 | tf_op jit(solution)/shard_map/all_gather | solution.py:78
  191.3 5.8 %reduce-scatter.6.cloned.1.call-done = f32[64,64]{1,0:T(8,128)} async-done(((f32[128,64]{1,0:T(8,128)}), f32[64,64]{1,0:T(8,128)}) %reduce-scatter.6.cloned.1.call-update) | async-done | bytes 16400 | tf_op jit(solution)/shard_map/reduce_scatter | solution.py:88
  197.9 39.3 %psum.31 = f32[64]{0:T(128)S(1)} all-reduce(f32[64]{0:T(128)S(1)} %multiply_reduce_fusion), channel_id=1, replica_groups=mesh['train'=16,'cand'=2] {'train','cand'}, use_global_device_ids=true, to_apply=%region_12.13 | all-reduce | flops 64 | bytes 512 | tf_op jit(solution)/shard_map/psum | solution.py:90
  237.8 4.6 %all_gather.15 = bf16[128,64]{1,0:T(8,128)(2,1)S(1)} all-gather(bf16[64,64]{1,0:T(8,128)(2,1)S(1)} %get-tuple-element.24), channel_id=1, replica_groups=mesh['train'=16,'cand'=2] {'cand'}, dimensions={0}, use_global_device_ids=true | all-gather | bytes 24576 | tf_op jit(solution)/shard_map/all_gather | solution.py:100
  243.3 2.7 fusion.5
  246.0 53.7 %reduce-scatter.8.cloned.1.call-done = f32[32,64]{1,0:T(8,128)} async-done(((f32[512,64]{1,0:T(8,128)}), f32[32,64]{1,0:T(8,128)}) %reduce-scatter.8.cloned.1.call-update) | async-done | bytes 8208 | tf_op jit(solution)/shard_map/reduce_scatter | solution.py:102
  299.8 1.6 convolution_add_fusion.2
  (60 shorter events, 10.5 us)
Async XLA Ops:
  7.2 19.1 %copy-start = (f32[8,4096]{1,0:T(8,128)S(1)}, f32[8,4096]{1,0:T(8,128)}, u32[]{:S(2)}) copy-start(f32[8,4096]{1,0:T(8,128)} %param.11) | copy-start | bytes 393220
  7.2 19.1 %copy-start.3 = (f32[4096]{0:T(1024)S(1)}, f32[4096]{0:T(1024)}, u32[]{:S(2)}) copy-start(f32[4096]{0:T(1024)} %param.12) | copy-start | bytes 49156
  7.2 79.5 %reduce-scatter.4.cloned.1.call-start = ((), (), s32[]{:S(2)}) async-start(), calls=%async_computation.3 | async-start | bytes 98304 | tf_op jit(solution)/shard_map/reduce_scatter | solution.py:88
  8.0 27.4 %copy-start.2 = (bf16[2048,64]{0,1:T(8,128)(2,1)S(1)}, bf16[2048,64]{0,1:T(8,128)(2,1)}, u32[]{:S(2)}) copy-start(bf16[2048,64]{0,1:T(8,128)(2,1)} %param.13) | copy-start | bytes 786436
  8.0 6.8 %collective-permute-start = (f32[8,64]{1,0:T(8,128)S(1)}, f32[8,64]{1,0:T(8,128)S(1)}, u32[]{:S(2)}, u32[]{:S(2)}) collective-permute-start(f32[8,64]{1,0:T(8,128)S(1)} %constant_dynamic-slice_fusion), channel_id=1, source_target_pairs={{0,2},{2,4},{4,6},{6,8},{8,10},{10,12},{12,14},{14,16},{16,18},{18... | collective-permute-start | bytes 6152 | tf_op jit(solution)/shard_map/ppermute | solution.py:17
  8.5 6.3 %collective-permute-start.8 = (f32[8,64]{1,0:T(8,128)S(1)}, f32[8,64]{1,0:T(8,128)S(1)}, u32[]{:S(2)}, u32[]{:S(2)}) collective-permute-start(f32[8,64]{1,0:T(8,128)S(1)} %constant_dynamic-slice_fusion), channel_id=1, source_target_pairs={{0,30},{2,0},{4,2},{6,4},{8,6},{10,8},{12,10},{14,12},{16,14},{18,... | collective-permute-start | bytes 6152 | tf_op jit(solution)/shard_map/ppermute | solution.py:19
  14.8 5.7 %collective-permute-start.1 = (f32[8,64]{1,0:T(8,128)S(1)}, f32[8,64]{1,0:T(8,128)S(1)}, u32[]{:S(2)}, u32[]{:S(2)}) collective-permute-start(f32[8,64]{1,0:T(8,128)S(1)} %collective-permute-done), channel_id=1, source_target_pairs={{0,2},{2,4},{4,6},{6,8},{8,10},{10,12},{12,14},{14,16},{16,18},{18... | collective-permute-start | bytes 6152 | tf_op jit(solution)/shard_map/ppermute | solution.py:17
  14.8 5.7 %collective-permute-start.9 = (f32[8,64]{1,0:T(8,128)S(1)}, f32[8,64]{1,0:T(8,128)S(1)}, u32[]{:S(2)}, u32[]{:S(2)}) collective-permute-start(f32[8,64]{1,0:T(8,128)S(1)} %collective-permute-done.8), channel_id=1, source_target_pairs={{0,30},{2,0},{4,2},{6,4},{8,6},{10,8},{12,10},{14,12},{16,14},{18,... | collective-permute-start | bytes 6152 | tf_op jit(solution)/shard_map/ppermute | solution.py:19
  20.5 5.7 %collective-permute-start.2 = (f32[8,64]{1,0:T(8,128)S(1)}, f32[8,64]{1,0:T(8,128)S(1)}, u32[]{:S(2)}, u32[]{:S(2)}) collective-permute-start(f32[8,64]{1,0:T(8,128)S(1)} %collective-permute-done.1), channel_id=1, source_target_pairs={{0,2},{2,4},{4,6},{6,8},{8,10},{10,12},{12,14},{14,16},{16,18},{18... | collective-permute-start | bytes 6152 | tf_op jit(solution)/shard_map/ppermute | solution.py:17
  20.5 10.3 %collective-permute-start.10 = (f32[8,64]{1,0:T(8,128)S(1)}, f32[8,64]{1,0:T(8,128)S(1)}, u32[]{:S(2)}, u32[]{:S(2)}) collective-permute-start(f32[8,64]{1,0:T(8,128)S(1)} %collective-permute-done.9), channel_id=1, source_target_pairs={{0,30},{2,0},{4,2},{6,4},{8,6},{10,8},{12,10},{14,12},{16,14},{18,... | collective-permute-start | bytes 6152 | tf_op jit(solution)/shard_map/ppermute | solution.py:19
  26.2 9.1 %collective-permute-start.3 = (f32[8,64]{1,0:T(8,128)S(1)}, f32[8,64]{1,0:T(8,128)S(1)}, u32[]{:S(2)}, u32[]{:S(2)}) collective-permute-start(f32[8,64]{1,0:T(8,128)S(1)} %collective-permute-done.2), channel_id=1, source_target_pairs={{0,2},{2,4},{4,6},{6,8},{8,10},{10,12},{12,14},{14,16},{16,18},{18... | collective-permute-start | bytes 6152 | tf_op jit(solution)/shard_map/ppermute | solution.py:17
  30.9 15.1 %copy-start.4 = (f32[64,64]{1,0:T(8,128)S(1)}, f32[64,64]{1,0:T(8,128)}, u32[]{:S(2)}) copy-start(f32[64,64]{1,0:T(8,128)} %param.10) | copy-start | bytes 49156
  30.9 15.0 %copy-start.7 = (f32[64]{0:T(128)S(1)}, f32[64]{0:T(128)}, u32[]{:S(2)}) copy-start(f32[64]{0:T(128)} %param.9) | copy-start | bytes 772
  30.9 11.5 %collective-permute-start.11 = (f32[8,64]{1,0:T(8,128)S(1)}, f32[8,64]{1,0:T(8,128)S(1)}, u32[]{:S(2)}, u32[]{:S(2)}) collective-permute-start(f32[8,64]{1,0:T(8,128)S(1)} %collective-permute-done.10), channel_id=1, source_target_pairs={{0,30},{2,0},{4,2},{6,4},{8,6},{10,8},{12,10},{14,12},{16,14},{18,... | collective-permute-start | bytes 6152 | tf_op jit(solution)/shard_map/ppermute | solution.py:19
  35.4 10.5 %collective-permute-start.4 = (f32[8,64]{1,0:T(8,128)S(1)}, f32[8,64]{1,0:T(8,128)S(1)}, u32[]{:S(2)}, u32[]{:S(2)}) collective-permute-start(f32[8,64]{1,0:T(8,128)S(1)} %collective-permute-done.3), channel_id=1, source_target_pairs={{0,2},{2,4},{4,6},{6,8},{8,10},{10,12},{12,14},{14,16},{16,18},{18... | collective-permute-start | bytes 6152 | tf_op jit(solution)/shard_map/ppermute | solution.py:17
  42.4 4.8 %collective-permute-start.12 = (f32[8,64]{1,0:T(8,128)S(1)}, f32[8,64]{1,0:T(8,128)S(1)}, u32[]{:S(2)}, u32[]{:S(2)}) collective-permute-start(f32[8,64]{1,0:T(8,128)S(1)} %collective-permute-done.11), channel_id=1, source_target_pairs={{0,30},{2,0},{4,2},{6,4},{8,6},{10,8},{12,10},{14,12},{16,14},{18,... | collective-permute-start | bytes 6152 | tf_op jit(solution)/shard_map/ppermute | solution.py:19
  45.9 5.7 %collective-permute-start.5 = (f32[8,64]{1,0:T(8,128)S(1)}, f32[8,64]{1,0:T(8,128)S(1)}, u32[]{:S(2)}, u32[]{:S(2)}) collective-permute-start(f32[8,64]{1,0:T(8,128)S(1)} %collective-permute-done.4), channel_id=1, source_target_pairs={{0,2},{2,4},{4,6},{6,8},{8,10},{10,12},{12,14},{14,16},{16,18},{18... | collective-permute-start | bytes 6152 | tf_op jit(solution)/shard_map/ppermute | solution.py:17
  47.2 5.7 %collective-permute-start.13 = (f32[8,64]{1,0:T(8,128)S(1)}, f32[8,64]{1,0:T(8,128)S(1)}, u32[]{:S(2)}, u32[]{:S(2)}) collective-permute-start(f32[8,64]{1,0:T(8,128)S(1)} %collective-permute-done.12), channel_id=1, source_target_pairs={{0,30},{2,0},{4,2},{6,4},{8,6},{10,8},{12,10},{14,12},{16,14},{18,... | collective-permute-start | bytes 6152 | tf_op jit(solution)/shard_map/ppermute | solution.py:19
  51.6 5.7 %collective-permute-start.6 = (f32[8,64]{1,0:T(8,128)S(1)}, f32[8,64]{1,0:T(8,128)S(1)}, u32[]{:S(2)}, u32[]{:S(2)}) collective-permute-start(f32[8,64]{1,0:T(8,128)S(1)} %collective-permute-done.5), channel_id=1, source_target_pairs={{0,2},{2,4},{4,6},{6,8},{8,10},{10,12},{12,14},{14,16},{16,18},{18... | collective-permute-start | bytes 6152 | tf_op jit(solution)/shard_map/ppermute | solution.py:17
  53.0 23.2 %collective-permute-start.14 = (f32[8,64]{1,0:T(8,128)S(1)}, f32[8,64]{1,0:T(8,128)S(1)}, u32[]{:S(2)}, u32[]{:S(2)}) collective-permute-start(f32[8,64]{1,0:T(8,128)S(1)} %collective-permute-done.13), channel_id=1, source_target_pairs={{0,30},{2,0},{4,2},{6,4},{8,6},{10,8},{12,10},{14,12},{16,14},{18,... | collective-permute-start | bytes 6152 | tf_op jit(solution)/shard_map/ppermute | solution.py:19
  57.4 18.8 %collective-permute-start.7 = (f32[8,64]{1,0:T(8,128)S(1)}, f32[8,64]{1,0:T(8,128)S(1)}, u32[]{:S(2)}, u32[]{:S(2)}) collective-permute-start(f32[8,64]{1,0:T(8,128)S(1)} %collective-permute-done.6), channel_id=1, source_target_pairs={{0,2},{2,4},{4,6},{6,8},{8,10},{10,12},{12,14},{14,16},{16,18},{18... | collective-permute-start | bytes 6152 | tf_op jit(solution)/shard_map/ppermute | solution.py:17
  78.4 118.7 %reduce-scatter.6.cloned.1.call-start = ((), (), s32[]{:S(2)}) async-start(), calls=%async_computation.4 | async-start | bytes 98304 | tf_op jit(solution)/shard_map/reduce_scatter | solution.py:88
  86.7 40.2 %copy-start.1 = (f32[64,64]{1,0:T(8,128)S(1)}, f32[64,64]{1,0:T(8,128)}, u32[]{:S(2)}) copy-start(f32[64,64]{1,0:T(8,128)} %reduce-scatter.4.cloned.1.call-done) | copy-start | bytes 49156
  190.6 109.2 %reduce-scatter.8.cloned.1.call-start = ((), (), s32[]{:S(2)}) async-start(), calls=%async_computation.5 | async-start | bytes 278528 | tf_op jit(solution)/shard_map/reduce_scatter | solution.py:102
  (2 other events, 9.9 us)
Sparse Core Ops, SparseCore 0:
  78.5 8.0 reduce-scatter.3
  190.7 6.2 reduce-scatter.5
  243.5 56.2 reduce-scatter.7
